TPU v7x, 32 devices: a whole 2x2x4 slice. The times are simulated.
32 devices in a mesh: bx: 8 (over y, x, core), by: 4 (over z).
Axes of the slice: x: 2, y: 2, z: 4, core: 2. Of those that a mesh axis runs over, the one named last changes fastest.
Arguments:
- right_sides: float32 [8, 4, 128, 768], P('bx', 'by'), may hold values from -6 to 6
- skeleton_order: int32 [8, 4, 4, 768], P('bx', 'by'), may hold values from 0 to 767, as said below
- interp_first: float32 [8, 4, 384, 384], P('bx', 'by'), may hold values from -0.15625 to 0.15625
- interp_second: float32 [8, 4, 384, 192], P('bx', 'by'), may hold values from -0.15625 to 0.15625
- interp_third: float32 [8, 4, 384, 96], P('bx', 'by'), may hold values from -0.15625 to 0.15625
- interp_fourth: float32 [8, 4, 384, 48], P('bx', 'by'), may hold values from -0.15625 to 0.15625
- inverse_first: float32 [8, 4, 384, 384], P('bx', 'by'), may hold values from -0.25 to 0.25
- inverse_second: float32 [8, 4, 384, 192], P('bx', 'by'), may hold values from -0.25 to 0.25
- inverse_third: float32 [8, 4, 384, 96], P('bx', 'by'), may hold values from -0.25 to 0.25
- inverse_fourth: float32 [8, 4, 384, 48], P('bx', 'by'), may hold values from -0.25 to 0.25
- couple_first: float32 [8, 4, 5, 384, 384], P('bx', 'by'), may hold values from -0.09375 to 0.09375
- couple_second: float32 [8, 4, 5, 384, 192], P('bx', 'by'), may hold values from -0.09375 to 0.09375
- couple_third: float32 [8, 4, 5, 384, 96], P('bx', 'by'), may hold values from -0.09375 to 0.09375
- couple_fourth: float32 [8, 4, 5, 384, 48], P('bx', 'by'), may hold values from -0.09375 to 0.09375
- root_inverse: float32 [8, 4, 384, 48], P('bx', 'by'), may hold values from -0.21875 to 0.21875
Outputs:
- solution: float32 [8, 4, 128, 768], P('bx', 'by')
Inputs may be any that keep to these rules, and one draw needn't show every extreme that they name: For every fine box and level l, skeleton_order[i, j, l, :] is a permutation of 0 to 767, the same at all fine boxes of one level-l box.
All inputs are finite; a program needn't handle non-finite values.
Results may differ from a plain program's by a relative error of at most 0.0003.
Values sent between devices are 32-bit elements; how exact they have to be, the bound alone decides.
A program may use at most 128 MiB of HBM per device.

v0:
```python
import jax
import jax.numpy as jnp
from jax import lax
from jax.sharding import PartitionSpec as P

HIGHEST = lax.Precision.HIGHEST
REACH = ((1, 1), (1, 2), (2, 2), (2, 4))


def from_behind(block, axis, distance):
    devices = range(lax.axis_size(axis))
    route = [(i - distance, i) for i in devices if i - distance in devices]
    return lax.ppermute(block, axis, route)


def swapped(x, axis, distance):
    return lax.ppermute(x, axis, [(i, i ^ 1 << distance) for i in range(lax.axis_size(axis))])


def merge_bit(step_index):
    return (0, lax.axis_size("by").bit_length() - 1, 1)[step_index]


def matmul(left_side, right_side):
    return jnp.dot(left_side, right_side, precision=HIGHEST, preferred_element_type=jnp.float32)


def along_x(field, distance):
    return from_behind(field, "bx", distance)


def along_y(field, distance):
    return from_behind(field, "by", distance)


def join_pair(own_part, partner, lower_flag):
    return jnp.where(
        lower_flag == 0,
        jnp.concatenate([own_part, partner], -1),
        jnp.concatenate([partner, own_part], -1),
    )


def body(
    right_sides,
    skeleton_order,
    interp_first,
    interp_second,
    interp_third,
    interp_fourth,
    inverse_first,
    inverse_second,
    inverse_third,
    inverse_fourth,
    couple_first,
    couple_second,
    couple_third,
    couple_fourth,
    root_inverse,
):
    index_x = lax.axis_index("bx")
    index_y = lax.axis_index("by")
    bit_flags = (index_y % 2, index_x % 2, index_y // 2 % 2)
    interps = [block[0, 0] for block in (interp_first, interp_second, interp_third, interp_fourth)]
    inverses = [
        block[0, 0] for block in (inverse_first, inverse_second, inverse_third, inverse_fourth)
    ]
    couples = [block[0, 0] for block in (couple_first, couple_second, couple_third, couple_fourth)]
    root_piece = root_inverse[0, 0]
    orders = skeleton_order[0, 0]
    skel_width = interps[0].shape[0]
    for level_index in (1, 2, 3):
        members = [interps[level_index][None], inverses[level_index][None], couples[level_index]]
        if level_index == 3:
            members.append(root_piece[None])
        joined = jnp.concatenate(members, 0)
        for step_index in range(level_index):
            partner = swapped(joined, ("bx", "by"), merge_bit(step_index))
            joined = join_pair(joined, partner, bit_flags[step_index])
        interps[level_index] = joined[0]
        inverses[level_index] = joined[1]
        couples[level_index] = joined[2:7]
        if level_index == 3:
            root_piece = joined[7]
    vector = right_sides[0, 0]
    stored = []
    skeleton = vector
    for level_index in range(4):
        reach_x, reach_y = REACH[level_index]
        piece_rank = jnp.int32(0)
        piece_width = interps[level_index].shape[-1]
        column_start = piece_rank * piece_width
        perm = orders[level_index]
        arranged = jnp.take(vector, perm, axis=1)
        skel_part = arranged[:, :skel_width]
        redund_part = arranged[:, skel_width:]
        redund_own = redund_part
        lowered = redund_own - matmul(skel_part, interps[level_index])
        solved = matmul(lowered, inverses[level_index])
        stacked = jnp.concatenate(
            [
                solved,
                along_x(solved, reach_x),
                along_x(solved, -reach_x),
                along_y(solved, reach_y),
                along_y(solved, -reach_y),
            ],
            1,
        )
        coupling = couples[level_index].reshape(5 * skel_width, piece_width)
        skel_own = skel_part
        skeleton = skel_own - matmul(stacked, coupling)
        stored.append((perm, solved, column_start, piece_width))
        if level_index < 3:
            partner = swapped(skeleton, ("bx", "by"), merge_bit(level_index))
            vector = join_pair(skeleton, partner, bit_flags[level_index])
    skel_value = matmul(skeleton, root_piece)
    for level_index in (3, 2, 1, 0):
        reach_x, reach_y = REACH[level_index]
        perm, solved, column_start, piece_width = stored[level_index]
        skel_own = skel_value
        partial_value = jnp.einsum("nc,krc->knr", skel_own, couples[level_index], precision=HIGHEST)
        update = (
            partial_value[0]
            + along_x(partial_value[1], -reach_x)
            + along_x(partial_value[2], reach_x)
            + along_y(partial_value[3], -reach_y)
            + along_y(partial_value[4], reach_y)
        )
        redund_sol = solved - jnp.einsum(
            "nc,rc->nr", update, inverses[level_index], precision=HIGHEST
        )
        redund_own = redund_sol
        skel_sol = skel_value - jnp.einsum(
            "nc,sc->ns", redund_own, interps[level_index], precision=HIGHEST
        )
        combined = jnp.concatenate([skel_sol, redund_sol], 1)
        box_width = perm.shape[0]
        inverse_perm = (
            jnp.zeros((box_width,), jnp.int32).at[perm].set(jnp.arange(box_width, dtype=jnp.int32))
        )
        vector = jnp.take(combined, inverse_perm, axis=1)
        if level_index > 0:
            skel_value = jnp.where(
                bit_flags[level_index - 1] == 0, vector[:, :skel_width], vector[:, skel_width:]
            )
    return vector[None, None]


def solution(mesh):
    in_specs = (
        P("bx", "by", None, None),
        P("bx", "by", None, None),
        P("bx", "by", None, None),
        P("bx", "by", None, None),
        P("bx", "by", None, None),
        P("bx", "by", None, None),
        P("bx", "by", None, None),
        P("bx", "by", None, None),
        P("bx", "by", None, None),
        P("bx", "by", None, None),
        P("bx", "by", None, None, None),
        P("bx", "by", None, None, None),
        P("bx", "by", None, None, None),
        P("bx", "by", None, None, None),
        P("bx", "by", None, None),
    )
    out_specs = P("bx", "by", None, None)
    return jax.shard_map(body, mesh=mesh, in_specs=in_specs, out_specs=out_specs, check_vma=False)
```

profile of v0, /device:TPU:19, one launch (start us, length us, event | category | flops | bytes accessed | tf_op | source)
XLA Modules:
  0.0 478.5 jit_solution(14092642810256241753)
XLA Ops:
  56.2 3.9 scatter_custom_fusion
  72.4 47.6 %collective-permute-done.4 = f32[128,384]{1,0:T(8,128)S(1)} collective-permute-done((f32[128,384]{1,0:T(8,128)S(1)}, f32[128,384]{1,0:T(8,128)S(1)}, u32[]{:S(2)}, u32[]{:S(2)}) %collective-permute-start.4) | collective-permute-done | bytes 196640 | tf_op jit(solution)/shard_map/ppermute | solution.py:17
  129.5 5.3 %maximum_select_fusion.5 = f32[8,384,96]{2,1,0:T(8,128)} fusion(f32[8,384,48]{2,1,0:T(8,128)} %copy.90, f32[8,384,48]{2,1,0:T(8,128)} %copy.89, pred[]{:T(512)S(6)} %eq.10), kind=kLoop, calls=%fused_computation.20 | loop fusion | flops 884736 | bytes 2359297 | tf_op jit(solution)/shard_map/jit(_where)/select_n | solution.py:37
  142.3 5.5 %maximum_select_fusion.4 = f32[7,384,192]{2,1,0:T(8,128)} fusion(f32[7,384,96]{2,1,0:T(8,128)} %copy.82, f32[5,384,96]{2,1,0:T(8,128)} %bitcast.215, f32[1,384,96]{2,1,0:T(8,128)S(1)} %bitcast.223, f32[1,384,96]{2,1,0:T(8,128)S(1)} %bitcast.221, pred[]{:T(512)S(6)} %eq.10), kind=kLoop, calls=%fused_computation.19 | loop fusion | flops 3612672 | bytes 4128769 | tf_op jit(solution)/shard_map/jit(_where)/select_n | solution.py:37
  154.4 6.8 %maximum_select_fusion.1 = f32[7,384,384]{2,1,0:T(8,128)S(1)} fusion(f32[7,384,192]{2,1,0:T(8,128)} %copy.74, f32[5,384,192]{2,1,0:T(8,128)} %bitcast.211, f32[1,384,192]{2,1,0:T(8,128)} %bitcast.219, f32[1,384,192]{2,1,0:T(8,128)S(1)} %bitcast.217, pred[]{:T(512)S(6)} %eq.10), kind=kLoop, calls=%fused_computation.13 | loop fusion | flops 7225344 | bytes 8257537 | tf_op jit(solution)/shard_map/jit(_where)/select_n | solution.py:37
  169.9 5.1 %collective-permute-start.9 = (f32[128,384]{1,0:T(8,128)S(1)}, f32[128,384]{1,0:T(8,128)S(1)}, u32[]{:S(2)}, u32[]{:S(2)}) collective-permute-start(f32[128,384]{1,0:T(8,128)S(1)} %get-tuple-element.33), channel_id=1, source_target_pairs={{2,0},{3,1},{6,4},{7,5},{10,8},{11,9},{14,12},{15,13},{18,16},{19,... | collective-permute-start | bytes 589832 | tf_op jit(solution)/shard_map/ppermute | solution.py:13
  177.1 5.4 %collective-permute-done.9 = f32[128,384]{1,0:T(8,128)S(1)} collective-permute-done((f32[128,384]{1,0:T(8,128)S(1)}, f32[128,384]{1,0:T(8,128)S(1)}, u32[]{:S(2)}, u32[]{:S(2)}) %collective-permute-start.9) | collective-permute-done | bytes 196640 | tf_op jit(solution)/shard_map/ppermute | solution.py:13
  193.4 6.2 %maximum_select_fusion.3 = f32[8,384,192]{2,1,0:T(8,128)} fusion(f32[8,384,96]{2,1,0:T(8,128)} %copy.94, f32[8,384,96]{2,1,0:T(8,128)} %maximum_select_fusion.5, pred[]{:T(512)S(6)} %eq.11), kind=kLoop, calls=%fused_computation.15 | loop fusion | flops 1769472 | bytes 4718593 | tf_op jit(solution)/shard_map/jit(_where)/select_n | solution.py:37
  216.6 5.8 %maximum_select_fusion.2 = f32[7,384,384]{2,1,0:T(8,128)S(1)} fusion(f32[7,384,192]{2,1,0:T(8,128)} %copy.85, f32[7,384,192]{2,1,0:T(8,128)} %maximum_select_fusion.4, pred[]{:T(512)S(6)} %eq.11), kind=kLoop, calls=%fused_computation.14 | loop fusion | flops 3096576 | bytes 8257537 | tf_op jit(solution)/shard_map/jit(_where)/select_n | solution.py:37
  239.3 5.1 %collective-permute-start.16 = (f32[128,384]{1,0:T(8,128)}, f32[128,384]{1,0:T(8,128)S(1)}, u32[]{:S(2)}, u32[]{:S(2)}) collective-permute-start(f32[128,384]{1,0:T(8,128)} %get-tuple-element.35), channel_id=1, source_target_pairs={{2,0},{3,1},{6,4},{7,5},{10,8},{11,9},{14,12},{15,13},{18,16},{19,... | collective-permute-start | bytes 589832 | tf_op jit(solution)/shard_map/ppermute | solution.py:13
  245.4 16.8 %collective-permute-done.15 = f32[128,384]{1,0:T(8,128)S(1)} collective-permute-done((f32[128,384]{1,0:T(8,128)}, f32[128,384]{1,0:T(8,128)S(1)}, u32[]{:S(2)}, u32[]{:S(2)}) %collective-permute-start.15) | collective-permute-done | bytes 196640 | tf_op jit(solution)/shard_map/ppermute | solution.py:13
  262.2 51.3 %collective-permute-done.16 = f32[128,384]{1,0:T(8,128)S(1)} collective-permute-done((f32[128,384]{1,0:T(8,128)}, f32[128,384]{1,0:T(8,128)S(1)}, u32[]{:S(2)}, u32[]{:S(2)}) %collective-permute-start.16) | collective-permute-done | bytes 196640 | tf_op jit(solution)/shard_map/ppermute | solution.py:13
  319.4 7.2 %collective-permute-done.17 = f32[128,384]{1,0:T(8,128)S(1)} collective-permute-done((f32[128,384]{1,0:T(8,128)S(1)}, f32[128,384]{1,0:T(8,128)S(1)}, u32[]{:S(2)}, u32[]{:S(2)}) %collective-permute-start.17) | collective-permute-done | bytes 196640 | tf_op jit(solution)/shard_map/ppermute | solution.py:17
  337.3 7.0 %maximum_select_fusion = f32[8,384,384]{2,1,0:T(8,128)S(1)} fusion(f32[8,384,192]{2,1,0:T(8,128)} %copy.97, f32[8,384,192]{2,1,0:T(8,128)} %maximum_select_fusion.3, pred[]{:T(512)S(6)} %eq.12), kind=kLoop, calls=%fused_computation.12 | loop fusion | flops 3538944 | bytes 9437185 | tf_op jit(solution)/shard_map/jit(_where)/select_n | solution.py:37
  353.4 3.9 collective-permute-done.22
  380.8 4.8 %convolution_bitcast_fusion.1 = f32[5,128,384]{1,2,0:T(8,128)S(1)} fusion(f32[7,384,384]{2,1,0:T(8,128)} %copy-done.2, f32[128,768]{1,0:T(8,128)S(1)} %select_bitcast_fusion.3, pred[]{:T(512)S(6)} %eq.12), kind=kOutput, calls=%fused_computation.24 | convolution fusion | flops 1132511232 | bytes 5505025 | tf_op jit(solution)/shard_map/nc,krc->knr/dot_general | solution.py:122
  387.6 5.0 %collective-permute-start.29 = (f32[128,384]{0,1:T(8,128)S(1)}, f32[128,384]{0,1:T(8,128)S(1)}, u32[]{:S(2)}, u32[]{:S(2)}) collective-permute-start(f32[128,384]{0,1:T(8,128)S(1)} %get-tuple-element.25), channel_id=1, source_target_pairs={{0,8},{4,12},{8,16},{12,20},{16,24},{20,28},{1,9},{5,13},{9,17},{1... | collective-permute-start | bytes 589832 | tf_op jit(solution)/shard_map/ppermute | solution.py:13
  392.6 5.0 %collective-permute-start.30 = (f32[128,384]{0,1:T(8,128)S(1)}, f32[128,384]{0,1:T(8,128)S(1)}, u32[]{:S(2)}, u32[]{:S(2)}) collective-permute-start(f32[128,384]{0,1:T(8,128)S(1)} %get-tuple-element.24), channel_id=1, source_target_pairs={{2,0},{3,1},{6,4},{7,5},{10,8},{11,9},{14,12},{15,13},{18,16},{19,... | collective-permute-start | bytes 589832 | tf_op jit(solution)/shard_map/ppermute | solution.py:13
  399.5 5.3 %collective-permute-done.30 = f32[128,384]{0,1:T(8,128)S(1)} collective-permute-done((f32[128,384]{0,1:T(8,128)S(1)}, f32[128,384]{0,1:T(8,128)S(1)}, u32[]{:S(2)}, u32[]{:S(2)}) %collective-permute-start.30) | collective-permute-done | bytes 196640 | tf_op jit(solution)/shard_map/ppermute | solution.py:13
  413.0 4.6 convolution_bitcast_fusion
  417.7 5.4 %collective-permute-start.32 = (f32[128,384]{0,1:T(8,128)S(1)}, f32[128,384]{0,1:T(8,128)S(1)}, u32[]{:S(2)}, u32[]{:S(2)}) collective-permute-start(f32[128,384]{0,1:T(8,128)S(1)} %get-tuple-element.18), channel_id=1, source_target_pairs={{4,0},{8,4},{12,8},{16,12},{20,16},{24,20},{28,24},{5,1},{9,5},{13... | collective-permute-start | bytes 589832 | tf_op jit(solution)/shard_map/ppermute | solution.py:13
  430.5 6.6 %collective-permute-done.34 = f32[128,384]{0,1:T(8,128)S(1)} collective-permute-done((f32[128,384]{0,1:T(8,128)S(1)}, f32[128,384]{0,1:T(8,128)S(1)}, u32[]{:S(2)}, u32[]{:S(2)}) %collective-permute-start.34) | collective-permute-done | bytes 196640 | tf_op jit(solution)/shard_map/ppermute | solution.py:13
  452.1 4.4 collective-permute-start.37
  456.5 5.6 %collective-permute-start.38 = (f32[128,384]{1,0:T(8,128)S(1)}, f32[128,384]{1,0:T(8,128)S(1)}, u32[]{:S(2)}, u32[]{:S(2)}) collective-permute-start(f32[128,384]{1,0:T(8,128)S(1)} %get-tuple-element.16), channel_id=1, source_target_pairs={{1,0},{2,1},{3,2},{5,4},{6,5},{7,6},{9,8},{10,9},{11,10},{13,12},{... | collective-permute-start | bytes 589832 | tf_op jit(solution)/shard_map/ppermute | solution.py:13
  (255 shorter events, 247.4 us)
Async XLA Ops:
  11.1 49.0 %collective-permute-start = (f32[128,384]{1,0:T(8,128)}, f32[128,384]{1,0:T(8,128)}, u32[]{:S(2)}, u32[]{:S(2)}) collective-permute-start(f32[128,384]{1,0:T(8,128)} %get-tuple-element.31), channel_id=1, source_target_pairs={{0,4},{4,8},{8,12},{12,16},{16,20},{20,24},{24,28},{1,5},{5,9},{9,... | collective-permute-start | bytes 589832 | tf_op jit(solution)/shard_map/ppermute | solution.py:13
  14.8 47.1 %collective-permute-start.1 = (f32[128,384]{1,0:T(8,128)}, f32[128,384]{1,0:T(8,128)}, u32[]{:S(2)}, u32[]{:S(2)}) collective-permute-start(f32[128,384]{1,0:T(8,128)} %get-tuple-element.31), channel_id=1, source_target_pairs={{4,0},{8,4},{12,8},{16,12},{20,16},{24,20},{28,24},{5,1},{9,5},{13... | collective-permute-start | bytes 589832 | tf_op jit(solution)/shard_map/ppermute | solution.py:13
  16.7 48.2 %collective-permute-start.2 = (f32[128,384]{1,0:T(8,128)}, f32[128,384]{1,0:T(8,128)}, u32[]{:S(2)}, u32[]{:S(2)}) collective-permute-start(f32[128,384]{1,0:T(8,128)} %get-tuple-element.31), channel_id=1, source_target_pairs={{0,1},{1,2},{2,3},{4,5},{5,6},{6,7},{8,9},{9,10},{10,11},{12,13},{... | collective-permute-start | bytes 589832 | tf_op jit(solution)/shard_map/ppermute | solution.py:13
  20.0 46.7 %collective-permute-start.3 = (f32[128,384]{1,0:T(8,128)}, f32[128,384]{1,0:T(8,128)}, u32[]{:S(2)}, u32[]{:S(2)}) collective-permute-start(f32[128,384]{1,0:T(8,128)} %get-tuple-element.31), channel_id=1, source_target_pairs={{1,0},{2,1},{3,2},{5,4},{6,5},{7,6},{9,8},{10,9},{11,10},{13,12},{... | collective-permute-start | bytes 589832 | tf_op jit(solution)/shard_map/ppermute | solution.py:13
  34.8 116.3 %collective-permute-start.5 = (f32[7,384,192]{1,2,0:T(8,128)}, f32[7,384,192]{1,2,0:T(8,128)}, u32[]{:S(2)}, u32[]{:S(2)}) collective-permute-start(f32[7,384,192]{1,2,0:T(8,128)} %copy.73), channel_id=1, source_target_pairs={{0,1},{1,0},{2,3},{3,2},{4,5},{5,4},{6,7},{7,6},{8,9},{9,8},{10,11... | collective-permute-start | bytes 6193160 | tf_op jit(solution)/shard_map/ppermute | solution.py:17
  60.2 66.6 %collective-permute-start.18 = (f32[8,384,48]{1,2,0:T(8,128)}, f32[8,384,48]{1,2,0:T(8,128)}, u32[]{:S(2)}, u32[]{:S(2)}) collective-permute-start(f32[8,384,48]{1,2,0:T(8,128)} %pad_maximum_fusion.2), channel_id=1, source_target_pairs={{0,1},{1,0},{2,3},{3,2},{4,5},{5,4},{6,7},{7,6},{8,9},{9,8},{10,11... | collective-permute-start | bytes 1769480 | tf_op jit(solution)/shard_map/ppermute | solution.py:17
  61.9 77.6 %collective-permute-start.11 = (f32[7,384,96]{1,2,0:T(8,128)}, f32[7,384,96]{1,2,0:T(8,128)}, u32[]{:S(2)}, u32[]{:S(2)}) collective-permute-start(f32[7,384,96]{1,2,0:T(8,128)} %copy.81), channel_id=1, source_target_pairs={{0,1},{1,0},{2,3},{3,2},{4,5},{5,4},{6,7},{7,6},{8,9},{9,8},{10,11... | collective-permute-start | bytes 3096584 | tf_op jit(solution)/shard_map/ppermute | solution.py:17
  71.7 48.3 %collective-permute-start.4 = (f32[128,384]{1,0:T(8,128)S(1)}, f32[128,384]{1,0:T(8,128)S(1)}, u32[]{:S(2)}, u32[]{:S(2)}) collective-permute-start(f32[128,384]{1,0:T(8,128)S(1)} %convolution_subtract_fusion.14), channel_id=1, source_target_pairs={{0,1},{1,0},{2,3},{3,2},{4,5},{5,4},{6,7},{7,6},{8,9},{9,8},{10,11... | collective-permute-start | bytes 589832 | tf_op jit(solution)/shard_map/ppermute | solution.py:17
  137.7 52.8 %collective-permute-start.19 = (f32[8,384,96]{1,2,0:T(8,128)}, f32[8,384,96]{1,2,0:T(8,128)}, u32[]{:S(2)}, u32[]{:S(2)}) collective-permute-start(f32[8,384,96]{1,2,0:T(8,128)} %copy.93), channel_id=1, source_target_pairs={{0,4},{1,5},{2,6},{3,7},{4,0},{5,1},{6,2},{7,3},{8,12},{9,13},{10,... | collective-permute-start | bytes 3538952 | tf_op jit(solution)/shard_map/ppermute | solution.py:17
  151.1 62.2 %collective-permute-start.12 = (f32[7,384,192]{1,2,0:T(8,128)}, f32[7,384,192]{1,2,0:T(8,128)}, u32[]{:S(2)}, u32[]{:S(2)}) collective-permute-start(f32[7,384,192]{1,2,0:T(8,128)} %copy.84), channel_id=1, source_target_pairs={{0,4},{1,5},{2,6},{3,7},{4,0},{5,1},{6,2},{7,3},{8,12},{9,13},{10,... | collective-permute-start | bytes 6193160 | tf_op jit(solution)/shard_map/ppermute | solution.py:17
  169.9 12.5 %collective-permute-start.9 = (f32[128,384]{1,0:T(8,128)S(1)}, f32[128,384]{1,0:T(8,128)S(1)}, u32[]{:S(2)}, u32[]{:S(2)}) collective-permute-start(f32[128,384]{1,0:T(8,128)S(1)} %get-tuple-element.33), channel_id=1, source_target_pairs={{2,0},{3,1},{6,4},{7,5},{10,8},{11,9},{14,12},{15,13},{18,16},{19,... | collective-permute-start | bytes 589832 | tf_op jit(solution)/shard_map/ppermute | solution.py:13
  184.6 21.5 %collective-permute-start.10 = (f32[128,384]{1,0:T(8,128)S(1)}, f32[128,384]{1,0:T(8,128)S(1)}, u32[]{:S(2)}, u32[]{:S(2)}) collective-permute-start(f32[128,384]{1,0:T(8,128)S(1)} %convolution_subtract_fusion.12), channel_id=1, source_target_pairs={{0,4},{1,5},{2,6},{3,7},{4,0},{5,1},{6,2},{7,3},{8,12},{9,13},{10,... | collective-permute-start | bytes 589832 | tf_op jit(solution)/shard_map/ppermute | solution.py:17
  203.0 130.9 %collective-permute-start.20 = (f32[8,384,192]{1,2,0:T(8,128)}, f32[8,384,192]{1,2,0:T(8,128)}, u32[]{:S(2)}, u32[]{:S(2)}) collective-permute-start(f32[8,384,192]{1,2,0:T(8,128)} %copy.96), channel_id=1, source_target_pairs={{0,2},{1,3},{2,0},{3,1},{4,6},{5,7},{6,4},{7,5},{8,10},{9,11},{10,... | collective-permute-start | bytes 7077896 | tf_op jit(solution)/shard_map/ppermute | solution.py:17
  225.8 18.6 %collective-permute-start.13 = (f32[128,384]{1,0:T(8,128)}, f32[128,384]{1,0:T(8,128)}, u32[]{:S(2)}, u32[]{:S(2)}) collective-permute-start(f32[128,384]{1,0:T(8,128)} %get-tuple-element.35), channel_id=1, source_target_pairs={{0,8},{4,12},{8,16},{12,20},{16,24},{20,28},{1,9},{5,13},{9,17},{1... | collective-permute-start | bytes 589832 | tf_op jit(solution)/shard_map/ppermute | solution.py:13
  233.2 12.2 %collective-permute-start.14 = (f32[128,384]{1,0:T(8,128)}, f32[128,384]{1,0:T(8,128)S(1)}, u32[]{:S(2)}, u32[]{:S(2)}) collective-permute-start(f32[128,384]{1,0:T(8,128)} %get-tuple-element.35), channel_id=1, source_target_pairs={{8,0},{12,4},{16,8},{20,12},{24,16},{28,20},{9,1},{13,5},{17,9},{2... | collective-permute-start | bytes 589832 | tf_op jit(solution)/shard_map/ppermute | solution.py:13
  237.7 24.4 %collective-permute-start.15 = (f32[128,384]{1,0:T(8,128)}, f32[128,384]{1,0:T(8,128)S(1)}, u32[]{:S(2)}, u32[]{:S(2)}) collective-permute-start(f32[128,384]{1,0:T(8,128)} %get-tuple-element.35), channel_id=1, source_target_pairs={{0,2},{1,3},{4,6},{5,7},{8,10},{9,11},{12,14},{13,15},{16,18},{17,... | collective-permute-start | bytes 589832 | tf_op jit(solution)/shard_map/ppermute | solution.py:13
  239.3 74.2 %collective-permute-start.16 = (f32[128,384]{1,0:T(8,128)}, f32[128,384]{1,0:T(8,128)S(1)}, u32[]{:S(2)}, u32[]{:S(2)}) collective-permute-start(f32[128,384]{1,0:T(8,128)} %get-tuple-element.35), channel_id=1, source_target_pairs={{2,0},{3,1},{6,4},{7,5},{10,8},{11,9},{14,12},{15,13},{18,16},{19,... | collective-permute-start | bytes 589832 | tf_op jit(solution)/shard_map/ppermute | solution.py:13
  315.7 10.8 %collective-permute-start.17 = (f32[128,384]{1,0:T(8,128)S(1)}, f32[128,384]{1,0:T(8,128)S(1)}, u32[]{:S(2)}, u32[]{:S(2)}) collective-permute-start(f32[128,384]{1,0:T(8,128)S(1)} %convolution_subtract_fusion.10), channel_id=1, source_target_pairs={{0,2},{1,3},{2,0},{3,1},{4,6},{5,7},{6,4},{7,5},{8,10},{9,11},{10,... | collective-permute-start | bytes 589832 | tf_op jit(solution)/shard_map/ppermute | solution.py:17
  385.7 13.8 %collective-permute-start.28 = (f32[128,384]{0,1:T(8,128)S(1)}, f32[128,384]{0,1:T(8,128)S(1)}, u32[]{:S(2)}, u32[]{:S(2)}) collective-permute-start(f32[128,384]{0,1:T(8,128)S(1)} %get-tuple-element.22), channel_id=1, source_target_pairs={{8,0},{12,4},{16,8},{20,12},{24,16},{28,20},{9,1},{13,5},{17,9},{2... | collective-permute-start | bytes 589832 | tf_op jit(solution)/shard_map/ppermute | solution.py:13
  387.6 11.9 %collective-permute-start.29 = (f32[128,384]{0,1:T(8,128)S(1)}, f32[128,384]{0,1:T(8,128)S(1)}, u32[]{:S(2)}, u32[]{:S(2)}) collective-permute-start(f32[128,384]{0,1:T(8,128)S(1)} %get-tuple-element.25), channel_id=1, source_target_pairs={{0,8},{4,12},{8,16},{12,20},{16,24},{20,28},{1,9},{5,13},{9,17},{1... | collective-permute-start | bytes 589832 | tf_op jit(solution)/shard_map/ppermute | solution.py:13
  392.6 12.2 %collective-permute-start.30 = (f32[128,384]{0,1:T(8,128)S(1)}, f32[128,384]{0,1:T(8,128)S(1)}, u32[]{:S(2)}, u32[]{:S(2)}) collective-permute-start(f32[128,384]{0,1:T(8,128)S(1)} %get-tuple-element.24), channel_id=1, source_target_pairs={{2,0},{3,1},{6,4},{7,5},{10,8},{11,9},{14,12},{15,13},{18,16},{19,... | collective-permute-start | bytes 589832 | tf_op jit(solution)/shard_map/ppermute | solution.py:13
  417.7 12.7 %collective-permute-start.32 = (f32[128,384]{0,1:T(8,128)S(1)}, f32[128,384]{0,1:T(8,128)S(1)}, u32[]{:S(2)}, u32[]{:S(2)}) collective-permute-start(f32[128,384]{0,1:T(8,128)S(1)} %get-tuple-element.18), channel_id=1, source_target_pairs={{4,0},{8,4},{12,8},{16,12},{20,16},{24,20},{28,24},{5,1},{9,5},{13... | collective-permute-start | bytes 589832 | tf_op jit(solution)/shard_map/ppermute | solution.py:13
  450.0 15.3 %collective-permute-start.36 = (f32[128,384]{1,0:T(8,128)S(1)}, f32[128,384]{1,0:T(8,128)S(1)}, u32[]{:S(2)}, u32[]{:S(2)}) collective-permute-start(f32[128,384]{1,0:T(8,128)S(1)} %get-tuple-element.14), channel_id=1, source_target_pairs={{4,0},{8,4},{12,8},{16,12},{20,16},{24,20},{28,24},{5,1},{9,5},{13... | collective-permute-start | bytes 589832 | tf_op jit(solution)/shard_map/ppermute | solution.py:13
  452.1 13.2 %collective-permute-start.37 = (f32[128,384]{1,0:T(8,128)S(1)}, f32[128,384]{1,0:T(8,128)S(1)}, u32[]{:S(2)}, u32[]{:S(2)}) collective-permute-start(f32[128,384]{1,0:T(8,128)S(1)} %get-tuple-element.17), channel_id=1, source_target_pairs={{0,4},{4,8},{8,12},{12,16},{16,20},{20,24},{24,28},{1,5},{5,9},{9,... | collective-permute-start | bytes 589832 | tf_op jit(solution)/shard_map/ppermute | solution.py:13
  (44 other events, 558.7 us)
where the time goes:
time: 486 us; the launch traced here: 478 us
  waiting for transfers between devices  154 us (32%)
  local copies, waits for them, and re-layouts  113 us (23%)
  starting transfers between devices  103 us (21%)
  other arithmetic  63.7 us (13%)
  matrix products  42.9 us (9%)
    ppermute x31, waiting for transfers between devices, from_behind(): return lax.ppermute(block, axis, route)  99.3 us
    ppermute x31, starting transfers between devices, from_behind(): return lax.ppermute(block, axis, route)  90.2 us
    ppermute x9, waiting for transfers between devices, swapped(): lax.ppermute(x, axis, [(i, i ^ 1 << distance) for i in range(lax.axis_siz...  54.9 us
    select_n x9, other arithmetic, join_pair(): jnp.where(lower_flag == 0, jnp.concatenate([own_part, partner], -1), jnp....  38.9 us
    unnamed x73, local copies, waits for them, and re-layouts  19.2 us
    ppermute x6, local copies, waits for them, and re-layouts, swapped(): lax.ppermute(x, axis, [(i, i ^ 1 << distance) for i in range(lax.axis_siz...  18.5 us
    dot_general x13, matrix products, matmul(): jnp.dot(left_side, right_side, precision=HIGHEST, preferred_element_type=...  17.8 us
    gather x8, local copies, waits for them, and re-layouts, body(): arranged = jnp.take(vector, perm, axis=1)  16.2 us
  transfers between devices with their start and end apart: 40, of which 15 were waited for; matrix products, arithmetic and copies ran while one was open for 30% of the time, Pallas kernels for 0%

commit v1 on v0

v1 whole, which is shorter than its diff:
```python
import functools

import jax
import jax.numpy as jnp
from jax import lax
from jax.experimental import pallas as pl
from jax.experimental.pallas import tpu as pltpu
from jax.sharding import PartitionSpec as P

REACH = ((1, 1), (1, 2), (2, 2), (2, 4))
F32 = jnp.float32
BF16 = jnp.bfloat16
MESH = pl.DeviceIdType.MESH
NN = (((1,), (0,)), ((), ()))
TN = (((0,), (0,)), ((), ()))
NT = (((1,), (1,)), ((), ()))


def halves(x):
    high = x.astype(BF16)
    return high, (x - high.astype(F32)).astype(BF16)


def product(a, b, dims):
    return lax.dot_general(a, b, dims, preferred_element_type=F32)


def dot3(a, b, dims):
    ah, al = halves(a)
    bh, bl = halves(b)
    return product(ah, bh, dims) + (product(ah, bl, dims) + product(al, bh, dims))


def pick_left(onehot, b, dims):
    bh, bl = halves(b)
    return product(onehot, bh, dims) + product(onehot, bl, dims)


def flips(m):
    return (m >> 1) & 1, (m & 1) | ((m >> 2 & 1) << 1)


def kernel(size_x, size_y, *refs):
    (rhs, order_col, order_row, t0, t1, t2, t3, g0, g1, g2, g3, k0, k1, k2, k3, root, out) = refs[:17]
    (ybuf, vbuf, qsend, qrecv, urecv1, urecv2, urecv3, xrecv1, xrecv2, xrecv3, xpart, tg1, tg2, tg3,
     n0, n1, n2, n3, abuf, ypart, tpart, ssend, send, recv) = refs[17:]
    interps, inverses, couples = (t0, t1, t2, t3), (g0, g1, g2, g3), (k0, k1, k2, k3)
    urecvs = (None, urecv1, urecv2, urecv3)
    xrecvs = (None, xrecv1, xrecv2, xrecv3)
    tgs = (None, tg1, tg2, tg3)
    ns = (n0, n1, n2, n3)
    skel = t0.shape[2]
    box = 2 * skel
    i, j = lax.axis_index("bx"), lax.axis_index("by")
    bits = (lax.rem(j, 2), lax.rem(i, 2), lax.rem(lax.div(j, 2), 2))
    ranks = [jnp.int32(0), bits[0], bits[0] + 2 * bits[1], bits[0] + 2 * bits[1] + 4 * bits[2]]

    def toggled(value, mask):
        for b in (0, 1):
            if mask >> b & 1:
                value = value + (1 << b) * (1 - 2 * lax.rem(lax.div(value, 1 << b), 2))
        return value

    def member(m):
        mx, my = flips(m)
        return (toggled(i, mx), toggled(j, my))

    def rank_of(level, m):
        rank = jnp.int32(0)
        for b in range(level):
            bit = bits[b]
            rank = rank + (1 << b) * ((1 - bit) if m >> b & 1 else bit)
        return rank

    count = [0]

    def slot():
        count[0] += 1
        return count[0] - 1

    def neighbour(level, k):
        rx, ry = REACH[level]
        bx, by = lax.div(i, rx), lax.div(j, ry)
        if k == 1:
            return i >= rx, (i - rx, j)
        if k == 2:
            return i + rx < size_x, (i + rx, j)
        if k == 3:
            return j >= ry, (i, j - ry)
        return j + ry < size_y, (i, j + ry)

    opposite = {1: 2, 2: 1, 3: 4, 4: 3}
    level_has = [[k for k in (1, 2, 3, 4) if (REACH[l][0] < size_x if k < 3 else REACH[l][1] < size_y)] for l in range(4)]

    def rcopy(src, dst, s, dev):
        return pltpu.make_async_remote_copy(src, dst, send.at[s], recv.at[s], device_id=dev, device_id_type=MESH)

    for level in range(4):
        for k in (1, 2, 3, 4):
            there, _ = neighbour(level, k)

            @pl.when(jnp.logical_not(there))
            def _():
                ybuf[level, pl.ds(k * skel, skel), :] = jnp.zeros((skel, ybuf.shape[2]), F32)
                qrecv[level, k - 1] = jnp.zeros((skel, ybuf.shape[2]), F32)

    barrier = pltpu.get_barrier_semaphore()
    for m in range(1, 8):
        pl.semaphore_signal(barrier, 1, device_id=member(m), device_id_type=MESH)
    total = jnp.int32(7)
    greeted = set()
    for level in range(4):
        for k in level_has[level]:
            key = (k, REACH[level][0] if k < 3 else REACH[level][1])
            if key in greeted:
                continue
            greeted.add(key)
            there, dev = neighbour(level, k)

            @pl.when(there)
            def _():
                pl.semaphore_signal(barrier, 1, device_id=dev, device_id_type=MESH)
            total = total + there.astype(jnp.int32)
    pl.semaphore_wait(barrier, total)

    pending = []

    t_copies = [[], [], [], []]

    def send_interp(level):
        for m in range(1, 1 << level):
            c = rcopy(interps[level].at[0, 0], tgs[level].at[ranks[level]], slot(), member(m))
            c.start()
            t_copies[level].append(c)
            pending.append(c)

    send_interp(1)

    def make_n(level):
        own = inverses[level][0, 0]
        cols = own.shape[1]
        if level == 0:
            acc = dot3(interps[0][0, 0], own, NN)
        else:
            tgs[level][ranks[level]] = interps[level][0, 0]
            for c in t_copies[level]:
                c.wait_recv()
            acc = jnp.zeros((skel, cols), F32)
            for q in range(1 << level):
                acc = acc + dot3(tgs[level][q], inverses[level][0, 0, q * cols:(q + 1) * cols, :], NN)
        ns[level][:skel, :] = -acc
        ns[level][skel:, :] = own

    def onehot_pt(level):
        lanes = lax.broadcasted_iota(jnp.int32, (box, box), 1)
        return jnp.where(lanes == order_col[:, level:level + 1], 1.0, 0.0).astype(BF16)

    def onehot_p(level):
        rows = lax.broadcasted_iota(jnp.int32, (box, box), 0)
        return jnp.where(rows == order_row[0, 0, level:level + 1, :], 1.0, 0.0).astype(BF16)

    for level in range(4):
        cols = interps[level].shape[3]
        rank = ranks[level]
        rows = pl.ds(pl.multiple_of(rank * cols, cols), cols)
        make_n(level)
        if level == 0:
            abuf[...] = pick_left(onehot_pt(0), rhs[0, 0], NT)
        else:
            abuf[...] = pick_left(onehot_pt(level), vbuf[level - 1], NN)
        y_own = dot3(ns[level][...], abuf[...], TN)
        ypart[level, :cols, :] = y_own
        ybuf[level, rows, :] = y_own
        gathers = []
        for m in range(1, 1 << level):
            c = rcopy(ypart.at[level, pl.ds(0, cols), :], ybuf.at[level, rows, :], slot(), member(m))
            c.start()
            gathers.append(c)
            pending.append(c)
        for c in gathers:
            c.wait_recv()
        for k in level_has[level]:
            s = slot()
            far = opposite[k]
            there, dev = neighbour(level, k)
            c = rcopy(ybuf.at[level, pl.ds(0, skel), :], ybuf.at[level, pl.ds(far * skel, skel), :], s, dev)

            @pl.when(there)
            def _():
                c.start()
            pending.append((there, c))
        base = count[0] - len(level_has[level])
        if level < 2:
            send_interp(level + 2)
        for k in level_has[level]:
            there, dev = neighbour(level, k)
            sent_as = level_has[level].index(opposite[k])
            c = rcopy(ybuf.at[level, pl.ds(0, skel), :], ybuf.at[level, pl.ds(k * skel, skel), :], base + sent_as, dev)

            @pl.when(there)
            def _():
                c.wait_recv()
        coupling = couples[level][0, 0].reshape(5 * skel, cols)
        s_own = abuf[rows, :] - dot3(coupling, ybuf[level], TN)
        ssend[level, :cols, :] = s_own
        wide = min(level + 1, 3)
        spot = pl.ds(pl.multiple_of(ranks[wide] * cols, cols), cols)
        vbuf[level, spot, :] = s_own
        gathers = []
        for m in range(1, 1 << wide):
            c = rcopy(ssend.at[level, pl.ds(0, cols), :], vbuf.at[level, spot, :], slot(), member(m))
            c.start()
            gathers.append(c)
            pending.append(c)
        for c in gathers:
            c.wait_recv()

    t_own = dot3(root[0, 0], vbuf[3, :skel, :], TN)

    for level in (3, 2, 1, 0):
        cols = interps[level].shape[3]
        rank = ranks[level]
        members = 1 << level
        rows = pl.ds(pl.multiple_of(rank * cols, cols), cols)
        tpart[:cols, :] = t_own
        q = dot3(couples[level][0, 0].reshape(5 * skel, cols), t_own, NN)
        qsend[level] = q
        base = count[0]
        for k in level_has[level]:
            s = slot()
            there, dev = neighbour(level, k)
            c = rcopy(qsend.at[level, pl.ds(k * skel, skel), :], qrecv.at[level, opposite[k] - 1], s, dev)

            @pl.when(there)
            def _():
                c.start()
            pending.append((there, c))
        for k in level_has[level]:
            there, dev = neighbour(level, k)
            sent_as = level_has[level].index(opposite[k])
            c = rcopy(qsend.at[level, pl.ds(k * skel, skel), :], qrecv.at[level, k - 1], base + sent_as, dev)

            @pl.when(there)
            def _():
                c.wait_recv()
        u = q[:skel] + ((qrecv[level, 0] + qrecv[level, 1]) + (qrecv[level, 2] + qrecv[level, 3]))
        if level > 0:
            qsend[level, :skel, :] = u
            gathers = []
            for m in range(1, members):
                far_rows = pl.ds(pl.multiple_of(rank_of(level, m) * cols, cols), cols)
                c = rcopy(qsend.at[level, far_rows, :], urecvs[level].at[m - 1], slot(), member(m))
                c.start()
                gathers.append(c)
                pending.append(c)
            for c in gathers:
                c.wait_recv()
            u_own = qsend[level, rows, :]
            for m in range(1, members):
                u_own = u_own + urecvs[level][m - 1]
        else:
            u_own = u
        y_own = ypart[level, :cols, :]
        comb = -dot3(ns[level][...], u_own, NN)
        low = dot3(interps[level][0, 0], y_own, NN)
        abuf[:skel, :] = comb[:skel] - low
        abuf[skel:, :] = comb[skel:]
        abuf[rows, :] = abuf[rows, :] + t_own
        rows_y = pl.ds(pl.multiple_of(skel + rank * cols, 8), cols)
        abuf[rows_y, :] = abuf[rows_y, :] + y_own
        if level > 0:
            xpart[level] = pick_left(onehot_p(level), abuf[...], NN)
            size = box // members
            gathers = []
            for m in range(1, members):
                far_rows = pl.ds(pl.multiple_of(rank_of(level, m) * size, size), size)
                c = rcopy(xpart.at[level, far_rows, :], xrecvs[level].at[m - 1], slot(), member(m))
                c.start()
                gathers.append(c)
                pending.append(c)
            for c in gathers:
                c.wait_recv()
            t_own = xpart[level, pl.ds(pl.multiple_of(rank * size, size), size), :]
            for m in range(1, members):
                t_own = t_own + xrecvs[level][m - 1]
        else:
            ch, cl = halves(abuf[...])
            pt = onehot_pt(0)
            out[0, 0] = product(ch, pt, TN) + product(cl, pt, TN)

    for item in pending:
        if isinstance(item, tuple):
            there, c = item

            @pl.when(there)
            def _():
                c.wait_send()
        else:
            item.wait_send()


def body(size_x, size_y, right_sides, skeleton_order, *weights):
    rows = right_sides.shape[2]
    box = right_sides.shape[3]
    skel = box // 2
    order_col = skeleton_order[0, 0].T
    vm = lambda *shape: pltpu.VMEM(shape, F32)
    widths = [w.shape[3] for w in weights[:4]]
    scratch = [
        vm(4, 5 * skel, rows), vm(4, box, rows), vm(4, 5 * skel, rows), vm(4, 4, skel, rows),
        vm(1, widths[1], rows), vm(3, widths[2], rows), vm(7, widths[3], rows),
        vm(1, box // 2, rows), vm(3, box // 4, rows), vm(7, box // 8, rows),
        vm(4, box, rows),
        vm(2, skel, widths[1]), vm(4, skel, widths[2]), vm(8, skel, widths[3]),
        vm(box, widths[0]), vm(box, widths[1]), vm(box, widths[2]), vm(box, widths[3]),
        vm(box, rows), vm(4, skel, rows), vm(skel, rows), vm(4, skel, rows),
        pltpu.SemaphoreType.DMA((128,)), pltpu.SemaphoreType.DMA((128,)),
    ]
    return pl.pallas_call(
        functools.partial(kernel, size_x, size_y),
        out_shape=jax.ShapeDtypeStruct(right_sides.shape, F32),
        in_specs=[pl.BlockSpec(memory_space=pltpu.VMEM)] * (3 + len(weights)),
        out_specs=pl.BlockSpec(memory_space=pltpu.VMEM),
        scratch_shapes=scratch,
        compiler_params=pltpu.CompilerParams(
            collective_id=0, has_side_effects=True, vmem_limit_bytes=60 * 2**20
        ),
    )(right_sides, order_col, skeleton_order, *weights)


def solution(mesh):
    four = P("bx", "by", None, None)
    five = P("bx", "by", None, None, None)
    in_specs = (four,) * 10 + (five,) * 4 + (four,)
    return jax.shard_map(
        functools.partial(body, mesh.shape["bx"], mesh.shape["by"]),
        mesh=mesh, in_specs=in_specs, out_specs=four, check_vma=False,
    )
```

time: 486 us -> 228 us (0.47)
  Pallas kernels: 0 us -> 207 us
  waiting for transfers between devices: 154 us -> 0 us
  starting transfers between devices: 103 us -> 0 us
  local copies, waits for them, and re-layouts: 113 us -> 18.6 us
  other arithmetic: 63.7 us -> 0 us
  matrix products: 42.9 us -> 0 us
    pallas_call x0 -> x1, Pallas kernels: none -> 207 us  [body(): pl.pallas_call(functools.partial(kernel, size_x, size_y), out_shape=jax.S...]
    ppermute x40 -> x0, waiting for transfers between devices: 154 us -> none  [the longest x31 99.3 us: from_behind(): return lax.ppermute(block, axis, route)]
    ppermute x40 -> x0, starting transfers between devices: 103 us -> none  [the longest x31 90.2 us: from_behind(): return lax.ppermute(block, axis, route)]
    select_n x25 -> x0, other arithmetic: 47.2 us -> none  [the longest x9 38.9 us: join_pair(): jnp.where(lower_flag == 0, jnp.concatenate([own_part, partner], -1), jnp....]
    dot_general x25 -> x0, matrix products: 42.9 us -> none  [the longest x13 17.8 us: matmul(): jnp.dot(left_side, right_side, precision=HIGHEST, preferred_element_type=...]
    gather x15 -> x0, local copies, waits for them, and re-layouts: 29 us -> none  [the longest x8 16.2 us: body(): arranged = jnp.take(vector, perm, axis=1)]
    ppermute x6 -> x0, local copies, waits for them, and re-layouts: 18.5 us -> none  [swapped(): lax.ppermute(x, axis, [(i, i ^ 1 << distance) for i in range(lax.axis_siz...]
    concatenate x11 -> x0, local copies, waits for them, and re-layouts: 15.2 us -> none  [the longest x3 8.86 us: body(): joined = jnp.concatenate(members, 0)]
  transfers between devices with their start and end apart: 40 -> 0, of which waited for: 15 -> 0; matrix products, arithmetic and copies ran while one was open for 30% -> 0% of each run, Pallas kernels for 0% -> 0%
where the time goes in v1:
time: 228 us; the launch traced here: 225 us
  Pallas kernels  207 us (91%)
  local copies, waits for them, and re-layouts  18.6 us (8%)
    pallas_call x1, Pallas kernels, body(): pl.pallas_call(functools.partial(kernel, size_x, size_y), out_shape=jax.S...  207 us
    unnamed x22, local copies, waits for them, and re-layouts  18.6 us

profile of v1, /device:TPU:19, one launch (start us, length us, event | category | flops | bytes accessed | tf_op | source)
XLA Modules:
  0.0 225.2 jit_solution(1960950630601139924)
XLA Ops:
  0.0 0.0 copy-start.4
  0.0 0.0 copy-start.1
  0.0 0.0 copy-start.3
  0.0 1.8 copy.18.refs_5_
  1.8 1.7 copy.19.refs_6_
  3.5 1.7 copy.21.refs_9_
  5.2 0.0 copy-start.2
  5.2 1.8 copy.22.refs_10_
  7.0 1.7 copy.26.refs_15_
  8.7 1.9 copy.17.refs_4_
  10.6 0.0 copy-done.3
  10.6 0.0 copy-start
  10.6 0.9 copy.20.refs_8_
  11.5 0.0 copy-done.4
  11.5 0.9 copy.16
  12.4 0.0 copy-done.1
  12.4 1.3 copy.24.refs_13_
  13.7 0.0 copy-done.2
  13.7 1.3 copy.25.refs_14_
  15.0 0.0 copy-done
  15.0 1.8 copy.23.refs_12_
  16.8 206.6 %shard_map.145 = f32[1,1,128,768]{3,2,1,0:T(8,128)} custom-call(f32[1,1,128,768]{3,2,1,0:T(8,128)} %refs_0_.1, s32[768,4]{1,0:T(8,128)} %bitcast.3, s32[1,1,4,768]{3,2,1,0:T(4,128)} %refs_2_.1, f32[1,1,384,384]{3,2,1,0:T(8,128)} %refs_3_.1, f32[1,1,384,192]{3,2,1,0:T(8,128)} %copy.17.refs_4_, f32[1,1,384,96]{3,2,1,0:T(8,128)} %copy.18.refs_5_, ...), custom_call_target="tpu_custom_call" | custom-call | tf_op jit(solution)/shard_map/pallas_call | solution.py:319
  223.5 1.8 copy.28
Async XLA Ops:
  0.0 11.5 %copy-start.4 = (s32[1,1,4,768]{3,2,1,0:T(4,128)S(1)}, s32[1,1,4,768]{3,2,1,0:T(4,128)}, u32[]{:S(2)}) copy-start(s32[1,1,4,768]{3,2,1,0:T(4,128)} %refs_2_.1) | copy-start | bytes 36868
  0.0 12.4 %copy-start.1 = (f32[1,1,5,384,96]{3,4,2,1,0:T(8,128)S(1)}, f32[1,1,5,384,96]{3,4,2,1,0:T(8,128)}, u32[]{:S(2)}) copy-start(f32[1,1,5,384,96]{3,4,2,1,0:T(8,128)} %param.27) | copy-start | bytes 2211844
  0.0 10.5 %copy-start.3 = (f32[1,1,384,192]{2,3,1,0:T(8,128)S(1)}, f32[1,1,384,192]{2,3,1,0:T(8,128)}, u32[]{:S(2)}) copy-start(f32[1,1,384,192]{2,3,1,0:T(8,128)} %param.22) | copy-start | bytes 884740
  5.2 8.5 %copy-start.2 = (f32[1,1,5,384,48]{3,4,2,1,0:T(8,128)S(1)}, f32[1,1,5,384,48]{3,4,2,1,0:T(8,128)}, u32[]{:S(2)}) copy-start(f32[1,1,5,384,48]{3,4,2,1,0:T(8,128)} %param.28) | copy-start | bytes 1105924
  10.6 4.5 %copy-start = (f32[1,1,5,384,192]{3,4,2,1,0:T(8,128)S(1)}, f32[1,1,5,384,192]{3,4,2,1,0:T(8,128)}, u32[]{:S(2)}) copy-start(f32[1,1,5,384,192]{3,4,2,1,0:T(8,128)} %param.26) | copy-start | bytes 4423684

commit v2 on v1

--- a/solution.py
+++ b/solution.py
@@ -43,7 +43,7 @@
 def kernel(size_x, size_y, *refs):
     (rhs, order_col, order_row, t0, t1, t2, t3, g0, g1, g2, g3, k0, k1, k2, k3, root, out) = refs[:17]
     (ybuf, vbuf, qsend, qrecv, urecv1, urecv2, urecv3, xrecv1, xrecv2, xrecv3, xpart, tg1, tg2, tg3,
-     n0, n1, n2, n3, abuf, ypart, tpart, ssend, send, recv) = refs[17:]
+     n0, n1, n2, n3, abuf, ypart, tpart, ssend, ptbuf, send, recv) = refs[17:]
     interps, inverses, couples = (t0, t1, t2, t3), (g0, g1, g2, g3), (k0, k1, k2, k3)
     urecvs = (None, urecv1, urecv2, urecv3)
     xrecvs = (None, xrecv1, xrecv2, xrecv3)
@@ -128,7 +128,7 @@
     t_copies = [[], [], [], []]
 
     def send_interp(level):
-        for m in range(1, 1 << level):
+        for m in [m for m in range(1, 1 << level) if not m & 2]:
             c = rcopy(interps[level].at[0, 0], tgs[level].at[ranks[level]], slot(), member(m))
             c.start()
             t_copies[level].append(c)
@@ -145,6 +145,16 @@
             tgs[level][ranks[level]] = interps[level][0, 0]
             for c in t_copies[level]:
                 c.wait_recv()
+            shared = []
+            for m in [m for m in range(1 << level) if not m & 2 and level > 1]:
+                block = rank_of(level, m)
+                held = interps[level].at[0, 0] if m == 0 else tgs[level].at[block]
+                c = rcopy(held, tgs[level].at[block], slot(), member(2))
+                c.start()
+                shared.append(c)
+                pending.append(c)
+            for c in shared:
+                c.wait_recv()
             acc = jnp.zeros((skel, cols), F32)
             for q in range(1 << level):
                 acc = acc + dot3(tgs[level][q], inverses[level][0, 0, q * cols:(q + 1) * cols, :], NN)
@@ -163,11 +173,11 @@
         cols = interps[level].shape[3]
         rank = ranks[level]
         rows = pl.ds(pl.multiple_of(rank * cols, cols), cols)
-        make_n(level)
         if level == 0:
+            make_n(0)
             abuf[...] = pick_left(onehot_pt(0), rhs[0, 0], NT)
         else:
-            abuf[...] = pick_left(onehot_pt(level), vbuf[level - 1], NN)
+            abuf[...] = pick_left(ptbuf[...], vbuf[level - 1], NN)
         y_own = dot3(ns[level][...], abuf[...], TN)
         ypart[level, :cols, :] = y_own
         ybuf[level, rows, :] = y_own
@@ -192,6 +202,9 @@
         base = count[0] - len(level_has[level])
         if level < 2:
             send_interp(level + 2)
+        if level < 3:
+            make_n(level + 1)
+            ptbuf[...] = onehot_pt(level + 1)
         for k in level_has[level]:
             there, dev = neighbour(level, k)
             sent_as = level_has[level].index(opposite[k])
@@ -235,6 +248,13 @@
             def _():
                 c.start()
             pending.append((there, c))
+        y_own = ypart[level, :cols, :]
+        abuf[:skel, :] = -dot3(interps[level][0, 0], y_own, NN)
+        abuf[skel:, :] = jnp.zeros_like(abuf[skel:, :])
+        abuf[rows, :] = abuf[rows, :] + t_own
+        rows_y = pl.ds(pl.multiple_of(skel + rank * cols, 8), cols)
+        abuf[rows_y, :] = y_own
+        ptbuf[...] = onehot_p(level) if level > 0 else onehot_pt(0)
         for k in level_has[level]:
             there, dev = neighbour(level, k)
             sent_as = level_has[level].index(opposite[k])
@@ -260,16 +280,10 @@
                 u_own = u_own + urecvs[level][m - 1]
         else:
             u_own = u
-        y_own = ypart[level, :cols, :]
         comb = -dot3(ns[level][...], u_own, NN)
-        low = dot3(interps[level][0, 0], y_own, NN)
-        abuf[:skel, :] = comb[:skel] - low
-        abuf[skel:, :] = comb[skel:]
-        abuf[rows, :] = abuf[rows, :] + t_own
-        rows_y = pl.ds(pl.multiple_of(skel + rank * cols, 8), cols)
-        abuf[rows_y, :] = abuf[rows_y, :] + y_own
+        abuf[...] = abuf[...] + comb
         if level > 0:
-            xpart[level] = pick_left(onehot_p(level), abuf[...], NN)
+            xpart[level] = pick_left(ptbuf[...], abuf[...], NN)
             size = box // members
             gathers = []
             for m in range(1, members):
@@ -285,7 +299,7 @@
                 t_own = t_own + xrecvs[level][m - 1]
         else:
             ch, cl = halves(abuf[...])
-            pt = onehot_pt(0)
+            pt = ptbuf[...]
             out[0, 0] = product(ch, pt, TN) + product(cl, pt, TN)
 
     for item in pending:
@@ -314,6 +328,7 @@
         vm(2, skel, widths[1]), vm(4, skel, widths[2]), vm(8, skel, widths[3]),
         vm(box, widths[0]), vm(box, widths[1]), vm(box, widths[2]), vm(box, widths[3]),
         vm(box, rows), vm(4, skel, rows), vm(skel, rows), vm(4, skel, rows),
+        pltpu.VMEM((box, box), BF16),
         pltpu.SemaphoreType.DMA((128,)), pltpu.SemaphoreType.DMA((128,)),
     ]
     return pl.pallas_call(

time: 228 us -> 210 us (0.921)
  Pallas kernels: 207 us -> 191 us
    pallas_call x1, Pallas kernels: 207 us -> 191 us  [body(): pl.pallas_call(functools.partial(kernel, size_x, size_y), out_shape=jax.S...]
where the time goes in v2:
time: 210 us; the launch traced here: 209 us
  Pallas kernels  191 us (91%)
  local copies, waits for them, and re-layouts  18.6 us (9%)
    pallas_call x1, Pallas kernels, body(): pl.pallas_call(functools.partial(kernel, size_x, size_y), out_shape=jax.S...  191 us
    unnamed x22, local copies, waits for them, and re-layouts  18.6 us

profile of v2, /device:TPU:19, one launch (start us, length us, event | category | flops | bytes accessed | tf_op | source)
XLA Modules:
  0.0 209.1 jit_solution(12694037128971414410)
XLA Ops:
  0.0 0.0 copy-start.4
  0.0 0.0 copy-start.1
  0.0 0.0 copy-start.3
  0.0 1.8 copy.18.refs_5_
  1.8 1.7 copy.19.refs_6_
  3.5 1.7 copy.21.refs_9_
  5.2 0.0 copy-start.2
  5.2 1.8 copy.22.refs_10_
  7.0 1.7 copy.26.refs_15_
  8.7 1.9 copy.17.refs_4_
  10.6 0.0 copy-done.3
  10.6 0.0 copy-start
  10.6 0.9 copy.20.refs_8_
  11.5 0.0 copy-done.4
  11.5 0.9 copy.16
  12.4 0.0 copy-done.1
  12.4 1.3 copy.24.refs_13_
  13.7 0.0 copy-done.2
  13.7 1.3 copy.25.refs_14_
  15.0 0.0 copy-done
  15.0 1.8 copy.23.refs_12_
  16.8 190.5 %shard_map.145 = f32[1,1,128,768]{3,2,1,0:T(8,128)} custom-call(f32[1,1,128,768]{3,2,1,0:T(8,128)} %refs_0_.1, s32[768,4]{1,0:T(8,128)} %bitcast.3, s32[1,1,4,768]{3,2,1,0:T(4,128)} %refs_2_.1, f32[1,1,384,384]{3,2,1,0:T(8,128)} %refs_3_.1, f32[1,1,384,192]{3,2,1,0:T(8,128)} %copy.17.refs_4_, f32[1,1,384,96]{3,2,1,0:T(8,128)} %copy.18.refs_5_, ...), custom_call_target="tpu_custom_call" | custom-call | tf_op jit(solution)/shard_map/pallas_call | solution.py:334
  207.3 1.8 copy.28
Async XLA Ops:
  0.0 11.5 %copy-start.4 = (s32[1,1,4,768]{3,2,1,0:T(4,128)S(1)}, s32[1,1,4,768]{3,2,1,0:T(4,128)}, u32[]{:S(2)}) copy-start(s32[1,1,4,768]{3,2,1,0:T(4,128)} %refs_2_.1) | copy-start | bytes 36868
  0.0 12.4 %copy-start.1 = (f32[1,1,5,384,96]{3,4,2,1,0:T(8,128)S(1)}, f32[1,1,5,384,96]{3,4,2,1,0:T(8,128)}, u32[]{:S(2)}) copy-start(f32[1,1,5,384,96]{3,4,2,1,0:T(8,128)} %param.27) | copy-start | bytes 2211844
  0.0 10.5 %copy-start.3 = (f32[1,1,384,192]{2,3,1,0:T(8,128)S(1)}, f32[1,1,384,192]{2,3,1,0:T(8,128)}, u32[]{:S(2)}) copy-start(f32[1,1,384,192]{2,3,1,0:T(8,128)} %param.22) | copy-start | bytes 884740
  5.2 8.5 %copy-start.2 = (f32[1,1,5,384,48]{3,4,2,1,0:T(8,128)S(1)}, f32[1,1,5,384,48]{3,4,2,1,0:T(8,128)}, u32[]{:S(2)}) copy-start(f32[1,1,5,384,48]{3,4,2,1,0:T(8,128)} %param.28) | copy-start | bytes 1105924
  10.6 4.5 %copy-start = (f32[1,1,5,384,192]{3,4,2,1,0:T(8,128)S(1)}, f32[1,1,5,384,192]{3,4,2,1,0:T(8,128)}, u32[]{:S(2)}) copy-start(f32[1,1,5,384,192]{3,4,2,1,0:T(8,128)} %param.26) | copy-start | bytes 4423684
